TPU v7x, 512 devices: a whole 4x8x8 slice. The times are simulated.
512 devices in a mesh: dp: 64 (over y, z_lo, core), tensor: 8 (over z_hi, x).
Axes of the slice: x: 4, y: 8, z: 8 (z_hi: 2, z_lo: 4; z = z_hi * 4 + z_lo), core: 2. Of those that a mesh axis runs over, the one named last changes fastest.
Arguments:
- layer_input: bfloat16 [2, 4096, 8192], P(None, ('dp', 'tensor')), may hold values from -6 to 6
- key_gradient_rows: bfloat16 [2, 4096, 1024], P(None, 'dp', 'tensor'), may hold values from -6 to 6
- key_block_matrix: bfloat16 [8, 6144, 128], P('tensor', 'dp'), may hold values from -0.09375 to 0.09375
- kept_rows: int32 [8, 48], replicated, may hold values from -1 to 63, as said below
Outputs:
- weight_grad: float32 [8, 6144, 128], P('tensor', 'dp')
- input_grad: bfloat16 [2, 4096, 8192], P(None, ('dp', 'tensor'))
Inputs may be any that keep to these rules, and one draw needn't show every extreme that they name: `kept_rows`: row h lists in ascending order the distinct blocks (of the 64 blocks of 128 input rows) that survive pruning for head h, then -1 in its unused slots. At most 48 blocks survive for one head and exactly 48 for some head; 256 blocks survive in all, at least one for every head.
All inputs are finite; a program needn't handle non-finite values.
Results may differ from a plain program's by a relative error of at most 0.005.
Values may be sent and summed in bfloat16 or wider, within the bound.
A program may use at most 64 MiB of HBM per device.

v0:
```python
import math

import jax
import jax.numpy as jnp
from jax import lax
from jax.sharding import PartitionSpec as P

MODEL_WIDTH = 8192
HEAD_WIDTH = 128
PRUNE_BLOCK_ROWS = 128
HEAD_BLOCK_LIMIT = 48
MICRO_BATCHES = 2


def local(layer_input, key_gradient_rows, key_block_matrix, kept_rows):
    my_head = lax.axis_index("tensor")
    groups = lax.axis_size("tensor")
    block_count = MODEL_WIDTH // PRUNE_BLOCK_ROWS
    own_rows = lax.dynamic_index_in_dim(kept_rows, my_head, 0, keepdims=False)
    alive = own_rows >= 0
    clipped = jnp.maximum(own_rows, 0)
    gathered_w = lax.all_gather(key_block_matrix, "dp", axis=1, tiled=True)
    blocks_w = gathered_w.reshape(HEAD_BLOCK_LIMIT, PRUNE_BLOCK_ROWS, HEAD_WIDTH) * alive[
        :, None, None
    ].astype(jnp.bfloat16)
    placing = (kept_rows[:, :, None] == jnp.arange(block_count)[None, None, :]).astype(jnp.bfloat16)
    accum = jnp.zeros((HEAD_BLOCK_LIMIT, PRUNE_BLOCK_ROWS, HEAD_WIDTH), jnp.float32)
    results = []
    for micro in range(MICRO_BATCHES):
        grads_here = key_gradient_rows[micro]
        group_x = lax.all_gather(layer_input[micro], "tensor", axis=0, tiled=True)
        picked = jnp.take(
            group_x.reshape(group_x.shape[0], block_count, PRUNE_BLOCK_ROWS), clipped, axis=1
        )
        product = jnp.einsum("gcb,gh->cbh", picked, grads_here, preferred_element_type=jnp.float32)
        accum = accum + product * alive[:, None, None].astype(jnp.float32)
        partial_value = jnp.einsum(
            "gh,cbh->gcb", grads_here, blocks_w, preferred_element_type=jnp.float32
        ).astype(jnp.bfloat16)
        partial_value = partial_value.reshape(
            grads_here.shape[0], 1, HEAD_BLOCK_LIMIT * PRUNE_BLOCK_ROWS
        )
        received = lax.all_to_all(partial_value, "tensor", split_axis=0, concat_axis=1, tiled=True)
        own_tokens = received.shape[0]
        received = received.reshape(own_tokens, groups, HEAD_BLOCK_LIMIT, PRUNE_BLOCK_ROWS)
        summed = jnp.einsum("tkcb,kcn->tnb", received, placing, preferred_element_type=jnp.float32)
        results.append(summed.reshape(own_tokens, MODEL_WIDTH).astype(jnp.bfloat16))
    owned = lax.psum_scatter(
        accum.reshape(HEAD_BLOCK_LIMIT * PRUNE_BLOCK_ROWS, HEAD_WIDTH),
        "dp",
        scatter_dimension=0,
        tiled=True,
    )
    scale = 1.0 / math.sqrt(MICRO_BATCHES * key_gradient_rows.shape[1] * lax.axis_size("dp"))
    weight_grad = (owned * scale)[None, :, :]
    return (weight_grad, jnp.stack(results))


def solution(mesh):
    placed = (
        P(None, ("dp", "tensor"), None),
        P(None, "dp", "tensor"),
        P("tensor", "dp", None),
        P(),
    )
    return jax.shard_map(
        local,
        mesh=mesh,
        in_specs=placed,
        out_specs=(P("tensor", "dp", None), P(None, ("dp", "tensor"), None)),
        check_vma=False,
    )
```

profile of v0, /device:TPU:6, one launch (start us, length us, event | category | flops | bytes accessed | tf_op | source)
XLA Modules:
  0.0 561.7 jit_solution(8836301085394832991)
XLA Ops:
  7.2 0.0 all-gather.10.cloned.1.call-start
  7.2 1.7 fusion.36
  8.9 0.0 all-gather.8.cloned.1.call-start
  9.0 0.7 all-gather.8.cloned.1.call-update
  9.7 0.7 all-gather.6.cloned.1.call-update
  10.4 0.0 reduce-scatter.2.cloned.1.call-start
  10.4 0.7 fusion.32
  11.1 0.7 compare_and_fusion
  11.8 72.0 %all-gather.10.cloned.1.call-done = bf16[1,64,8192]{2,1,0:T(8,128)(2,1)} async-done(((bf16[1,8,8192]{2,1,0:T(8,128)(2,1)}), bf16[1,64,8192]{2,1,0:T(8,128)(2,1)}) %all-gather.10.cloned.1.call-update) | async-done | bytes 1048592 | tf_op jit(solution)/shard_map/all_gather | solution.py:31
  83.8 1.5 copy.31
  85.3 0.7 copy.17
  86.0 64.4 %all-gather.8.cloned.1.call-done = bf16[1,64,8192]{2,1,0:T(8,128)(2,1)} async-done(((bf16[1,8,8192]{2,1,0:T(8,128)(2,1)}), bf16[1,64,8192]{2,1,0:T(8,128)(2,1)}) %all-gather.8.cloned.1.call-update) | async-done | bytes 1048592 | tf_op jit(solution)/shard_map/all_gather | solution.py:31
  150.5 1.5 copy.30
  152.0 0.7 copy.16
  152.7 0.7 gather_fusion.1
  153.4 0.7 gather_fusion
  154.1 0.8 fusion.11
  154.9 2.8 add_multiply_fusion
  157.7 0.1 broadcast_bitcast_fusion
  157.8 109.0 %all-gather.6.cloned.1.call-done = bf16[1,6144,128]{2,1,0:T(8,128)(2,1)} async-done(((bf16[1,96,128]{2,1,0:T(8,128)(2,1)}), bf16[1,6144,128]{2,1,0:T(8,128)(2,1)}) %all-gather.6.cloned.1.call-update) | async-done | bytes 1572880 | tf_op jit(solution)/shard_map/all_gather | solution.py:22
  266.8 2.1 broadcast_multiply_fusion
  268.9 0.7 fusion.1
  269.6 1.4 copy.21
  271.0 4.4 reshape.124
  275.4 0.5 broadcast.58
  275.9 6.2 %reduce = bf16[64,6144]{1,0:T(8,128)(2,1)} reduce(bf16[64,1,6144]{2,1,0:T(2,128)(2,1)S(1)} %reshape.124, bf16[]{:T(256)} %broadcast.58), dimensions={1}, to_apply=%reshape.124.reduce_sub_computation | reduce | bytes 1572866 | tf_op jit(solution)/shard_map/reshape | solution.py:40
  282.2 3.2 reshape.126
  285.3 8.2 %all-to-all-start.1 = ((bf16[8,2,24576]{2,1,0:T(2,128)(2,1)}), bf16[8,2,24576]{2,1,0:T(2,128)(2,1)S(1)}, u32[]{:S(2)}, u32[]{:S(2)}) async-start(bf16[8,2,24576]{2,1,0:T(2,128)(2,1)} %reshape.126), calls=%async_computation.2 | async-start | bytes 1572864 | tf_op jit(solution)/shard_map/all_to_all | solution.py:43
  293.6 0.7 fusion
  294.2 1.4 copy.18
  295.6 4.4 reshape.122
  300.1 5.4 reduce.1
  305.4 1.7 reshape.128
  307.1 5.2 all-to-all-done.1
  312.3 4.9 all-to-all-start
  317.2 0.8 reshape.127
  318.0 0.4 copy.44
  318.5 0.2 copy-done.1
  318.7 0.4 fusion.4
  319.2 0.1 convert_element_type.78
  319.2 13.0 %all-to-all-done = bf16[8,2,24576]{2,1,0:T(2,128)(2,1)S(1)} async-done(((bf16[8,2,24576]{2,1,0:T(2,128)(2,1)}), bf16[8,2,24576]{2,1,0:T(2,128)(2,1)S(1)}, u32[]{:S(2)}, u32[]{:S(2)}) %all-to-all-start) | async-done | bytes 786464 | tf_op jit(solution)/shard_map/all_to_all | solution.py:43
  332.2 0.8 reshape.129
  333.0 0.4 copy.45
  333.5 0.4 fusion.5
  333.9 0.1 convert_element_type.73
  334.0 0.7 pad_maximum_fusion
  334.7 219.0 %reduce-scatter.2.cloned.1.call-done = f32[96,128]{1,0:T(8,128)} async-done(((f32[6144,128]{1,0:T(8,128)}), f32[96,128]{1,0:T(8,128)}) %reduce-scatter.2.cloned.1.call-update) | async-done | bytes 49168 | tf_op jit(solution)/shard_map/reduce_scatter | solution.py:48
  553.7 1.4 multiply_bitcast_fusion
  (7 shorter events, 0.1 us)
Async XLA Ops:
  7.2 76.7 %all-gather.10.cloned.1.call-start = ((), (), s32[]{:S(2)}) async-start(), calls=%async_computation.6 | async-start | bytes 1179648 | tf_op jit(solution)/shard_map/all_gather | solution.py:31
  8.9 141.6 %all-gather.8.cloned.1.call-start = ((), (), s32[]{:S(2)}) async-start(), calls=%async_computation.5 | async-start | bytes 1179648 | tf_op jit(solution)/shard_map/all_gather | solution.py:31
  9.7 257.1 %all-gather.6.cloned.1.call-start = ((), (), s32[]{:S(2)}) async-start(), calls=%async_computation.4 | async-start | bytes 1597440 | tf_op jit(solution)/shard_map/all_gather | solution.py:22
  10.4 543.3 %reduce-scatter.2.cloned.1.call-start = ((), (), s32[]{:S(2)}) async-start(), calls=%async_computation.3 | async-start | bytes 3194880 | tf_op jit(solution)/shard_map/reduce_scatter | solution.py:48
  152.7 1.4 copy-start
  285.3 27.0 %all-to-all-start.1 = ((bf16[8,2,24576]{2,1,0:T(2,128)(2,1)}), bf16[8,2,24576]{2,1,0:T(2,128)(2,1)S(1)}, u32[]{:S(2)}, u32[]{:S(2)}) async-start(bf16[8,2,24576]{2,1,0:T(2,128)(2,1)} %reshape.126), calls=%async_computation.2 | async-start | bytes 1572864 | tf_op jit(solution)/shard_map/all_to_all | solution.py:43
  312.3 19.9 %all-to-all-start = ((bf16[8,2,24576]{2,1,0:T(2,128)(2,1)}), bf16[8,2,24576]{2,1,0:T(2,128)(2,1)S(1)}, u32[]{:S(2)}, u32[]{:S(2)}) async-start(bf16[8,2,24576]{2,1,0:T(2,128)(2,1)} %reshape.128), calls=%async_computation.1 | async-start | bytes 1572864 | tf_op jit(solution)/shard_map/all_to_all | solution.py:43
  318.0 0.7 copy-start.1
Sparse Core Ops, SparseCore 0:
  11.8 72.0 all-gather.9
  87.0 63.3 all-gather.7
  152.6 114.1 all-gather.5
  269.4 284.2 reduce-scatter.1
where the time goes:
time: 562 us
  waiting for transfers between devices  484 us (86%)
  local copies, waits for them, and re-layouts  27.4 us (5%)
  other arithmetic  17.2 us (3%)
  between operations  14 us (2%)
  starting transfers between devices  13.3 us (2%)
  matrix products  5.81 us (1%)
    reduce_scatter x1, waiting for transfers between devices, local(): lax.psum_scatter(accum.reshape(HEAD_BLOCK_LIMIT * PRUNE_BLOCK_ROWS, HEAD_...  219 us
    all_gather x2, waiting for transfers between devices, local(): group_x = lax.all_gather(layer_input[micro], 'tensor', axis=0, tiled=True)  136 us
    all_gather x1, waiting for transfers between devices, local(): gathered_w = lax.all_gather(key_block_matrix, 'dp', axis=1, tiled=True)  109 us
    all_to_all x2, waiting for transfers between devices, local(): lax.all_to_all(partial_value, 'tensor', split_axis=0, concat_axis=1, tile...  18.1 us
    all_to_all x2, starting transfers between devices, local(): lax.all_to_all(partial_value, 'tensor', split_axis=0, concat_axis=1, tile...  13.1 us
    reshape x2, other arithmetic, local(): partial_value.reshape(grads_here.shape[0], 1, HEAD_BLOCK_LIMIT * PRUNE_BL...  11.6 us
  transfers between devices with their start and end apart: 6, of which 6 were waited for; matrix products, arithmetic and copies ran while one was open for 8% of the time, Pallas kernels for 0%

commit v1 on v0

v1 whole, which is shorter than its diff:
```python
import math

import jax
import jax.numpy as jnp
from jax import lax
from jax.experimental import pallas as pl
from jax.experimental.pallas import tpu as pltpu
from jax.sharding import PartitionSpec as P

MODEL_WIDTH = 8192
HEAD_WIDTH = 128
BLOCK = 128
SLOTS = 48
BLOCKS = MODEL_WIDTH // BLOCK
MICRO = 2
N = 8
XN = 4
SHARD = SLOTS * BLOCK // 64
HALF = SHARD // 2
UNIT = 16
PER = BLOCK // UNIT
SHARD_UNITS = SHARD // UNIT
HEAD_UNITS = SLOTS * PER
HEAD_STRIDE = HEAD_UNITS + PER
DENSE_STRIDE = BLOCKS * PER + PER
OWN = 16
GROUP = MODEL_WIDTH // 4
MESH = pl.DeviceIdType.MESH
OFFSETS = (0, 1, -1, 2, -2, 3, -3, 4)
AT = {offset: index for index, offset in enumerate(OFFSETS)}
DIRECTIONS = ((0, 1), (1, -1))
X_ORDER = ((0, 1, 2, 3, 0, 1), (2, 3, 0, 1, 2, 3))
f32, bf16 = jnp.float32, jnp.bfloat16


def wrap(value, size):
    return lax.rem(value + size, size)


def kernel(
    kept, slot_of, x_in, k_in, w_in, w_out, x_out,
    w_all, x_all, k_raw, k_hop, k_cat, dense, part, got, total, got2, send2, og, xr, xa,
    local_sem, a_send, a_recv, b_send, b_recv, pw_send, pw_recv, px_send, px_recv, pk_send, pk_recv,
    x_send, x_recv, kc_send, kc_recv, r_send, r_recv, s_send, s_recv, o_send, o_recv,
):
    dp, tp = lax.axis_index("dp"), lax.axis_index("tensor")
    y, zl, core = dp // 8, lax.rem(dp // 2, 4), lax.rem(dp, 2)
    zh, xx = tp // 4, lax.rem(tp, 4)
    z = zh * 4 + zl
    a = y + core * (z - y)
    b = z + core * (y - z)

    def device(y_, z_, core_, x_):
        return (y_ * 8 + lax.rem(z_, 4) * 2 + core_, (z_ // 4) * 4 + x_)

    def device_ab(a_, b_):
        return device(a_ + core * (b_ - a_), b_ + core * (a_ - b_), core, xx)

    a_at = {o: wrap(a + o, N) for o in OFFSETS}
    b_at = {o: wrap(b + o, N) for o in OFFSETS}

    def y_rows(y_):
        return y_ * (768 // UNIT)

    def z_rows(z_):
        return (z_ // 4) * HEAD_STRIDE + PER + lax.rem(z_, 4) * (192 // UNIT)

    a_rows = {o: y_rows(v) + core * (z_rows(v) - y_rows(v)) + core * SHARD_UNITS for o, v in a_at.items()}
    b_rows = {o: z_rows(v) + core * (y_rows(v) - z_rows(v)) for o, v in b_at.items()}
    to_a = {d: device_ab(a_at[d], b) for d in (1, -1)}
    to_b = {d: device_ab(a, b_at[d]) for d in (1, -1)}
    to_z = {d: device(y, wrap(z + d, N), core, xx) for d in (1, -1)}
    to_x = {d: device(y, z, core, wrap(xx + d, XN)) for d in (1, -1)}
    to_y = {d: device(wrap(y + d, N), z, core, xx) for d in (1, -1)}
    partner = device(y, z, 1 - core, xx)

    barrier = pltpu.get_barrier_semaphore()
    for there in (to_y[1], to_y[-1], to_z[1], to_z[-1], to_x[1], to_x[-1], partner):
        pl.semaphore_signal(barrier, inc=1, device_id=there, device_id_type=MESH)

    def remote(src, dst, send, recv, there):
        return pltpu.make_async_remote_copy(
            src_ref=src, dst_ref=dst, send_sem=send, recv_sem=recv, device_id=there, device_id_type=MESH
        )

    def piece(oa, ob, half=None):
        row = a_rows[oa] + b_rows[ob]
        if half is None:
            return w_all.at[pl.ds(row, SHARD_UNITS)]
        return w_all.at[pl.ds(row + half * (SHARD_UNITS // 2), SHARD_UNITS // 2)]

    def ring_offset(d, hop):
        return 4 if hop == 4 else -d * hop

    def a_copy(i, d, hop):
        offset = -d * (hop - 1)
        half = i if hop == 4 else None
        src = w_in if hop == 1 else piece(offset, 0, half)
        return remote(src, piece(offset, 0, half), a_send.at[i, hop - 1], a_recv.at[i, hop - 1], to_a[d])

    def b_copy(oa, i, d, hop):
        offset = -d * (hop - 1)
        half = i if hop == 4 else None
        src = w_in if hop == 1 and oa == 0 else piece(oa, offset, half)
        j = AT[oa]
        return remote(
            src, piece(oa, offset, half), b_send.at[j, i, hop - 1], b_recv.at[j, i, hop - 1], to_b[d]
        )

    def share(oa, ob, half=None, src=None):
        ref = piece(oa, ob, half)
        remote(ref if src is None else src, ref, pw_send, pw_recv, partner).start()

    def x_rows(core_, x_):
        return pl.ds(pl.multiple_of(core_ * 64 + x_ * OWN, OWN), OWN)

    def x_columns(group):
        return pl.ds(group * GROUP, GROUP)

    def x_copy(i, d, n):
        columns = x_columns(X_ORDER[i][n])
        if n < 4:
            src, origin = x_in.at[:, columns], xx
        else:
            origin = wrap(xx - d, XN)
            src = x_all.at[x_rows(core, origin), columns]
        return remote(
            src, x_all.at[x_rows(core, origin), columns], x_send.at[i, n], x_recv.at[i, n], to_x[d]
        )

    def share_x(i, d, n):
        origin = wrap(xx - d, XN) if n < 4 else wrap(xx - 2 * d, XN)
        ref = x_all.at[x_rows(core, origin), x_columns(X_ORDER[i][n])]
        remote(ref, ref, px_send, px_recv, partner).start()

    def k_copy(i, d, hop):
        if hop == 1:
            src = k_in.at[i, pl.ds(pl.multiple_of((1 - zh) * 32, 32), 32)]
        else:
            src = k_hop.at[i, hop - 2]
        if hop == 4:
            dst = k_raw.at[core, 1 - wrap(z + d, N) // 4, i]
        else:
            dst = k_hop.at[i, hop - 1]
        return remote(src, dst, kc_send.at[i, hop - 1], kc_recv.at[i, hop - 1], to_z[d])

    def k_share(own):
        if own:
            src = k_in.at[:, pl.ds(pl.multiple_of(zh * 32, 32), 32)]
            return remote(src, k_raw.at[core, zh], pk_send.at[0], pk_recv.at[0], partner)
        ref = k_raw.at[core, 1 - zh]
        return remote(ref, ref, pk_send.at[1], pk_recv.at[1], partner)

    local = [
        pltpu.make_async_copy(w_in, piece(0, 0), local_sem.at[0]),
        pltpu.make_async_copy(x_in, x_all.at[x_rows(core, xx)], local_sem.at[1]),
        pltpu.make_async_copy(
            k_in.at[:, pl.ds(pl.multiple_of(zh * 32, 32), 32)], k_raw.at[core, zh], local_sem.at[2]
        ),
    ]
    for copy in local:
        copy.start()
    for head in range(2):
        w_all[pl.ds(head * HEAD_STRIDE, PER)] = jnp.zeros((PER, UNIT, HEAD_WIDTH), bf16)
        dense[pl.ds(head * DENSE_STRIDE, PER)] = jnp.zeros((PER, UNIT, HEAD_WIDTH), bf16)

    pl.semaphore_wait(barrier, 7)

    for i, d in DIRECTIONS:
        a_copy(i, d, 1).start()
        b_copy(0, i, d, 1).start()
        k_copy(i, d, 1).start()
    for n in range(4):
        for i, d in DIRECTIONS:
            x_copy(i, d, n).start()
    share(0, 0, src=w_in)
    k_share(True).start()
    remote(x_in, x_all.at[x_rows(core, xx)], px_send, px_recv, partner).start()

    def a_arrival(step):
        for i, d in DIRECTIONS:
            a_copy(i, d, step).wait_recv()
            if step < 4:
                a_copy(i, d, step + 1).start()
                for i2, d2 in DIRECTIONS:
                    b_copy(-d * step, i2, d2, 1).start()
                share(-d * step, 0)
        if step == 4:
            for i2, d2 in DIRECTIONS:
                b_copy(4, i2, d2, 1).start()
            share(4, 0)

    def b_arrival(oa, hop):
        for i, d in DIRECTIONS:
            b_copy(oa, i, d, hop).wait_recv()
            if hop < 4:
                b_copy(oa, i, d, hop + 1).start()
                share(oa, -d * hop)
            else:
                share(oa, 4, i)

    for step in range(1, 9):
        if step <= 4:
            a_arrival(step)
        for oa in OFFSETS:
            hop = step - abs(oa)
            if 1 <= hop <= 4:
                b_arrival(oa, hop)
        if step <= 4:
            for i, d in DIRECTIONS:
                k_copy(i, d, step).wait_recv()
                if step < 4:
                    k_copy(i, d, step + 1).start()
            if step == 4:
                k_share(False).start()
        if step in (2, 3, 5, 6):
            n = {2: 0, 3: 1, 5: 2, 6: 3}[step]
            for i, d in DIRECTIONS:
                x_copy(i, d, n).wait_recv()
                if n < 2:
                    x_copy(i, d, n + 4).start()
                share_x(i, d, n)
    for n in (4, 5):
        for i, d in DIRECTIONS:
            x_copy(i, d, n).wait_recv()
            share_x(i, d, n)

    for copy in local:
        copy.wait()
    k_share(True).wait()
    k_share(False).wait()
    for core_ in range(2):
        for head in range(2):
            raw = k_raw[core_, head].astype(f32)
            rows = [raw[m, x_ * 8:x_ * 8 + 8] for x_ in range(XN) for m in range(MICRO)]
            k_cat[core_ * 64:core_ * 64 + 64, head * 128:head * 128 + 128] = jnp.concatenate(
                rows, axis=0
            ).astype(bf16)
    x_shared = x_all.at[pl.ds(0, 64)]
    remote(x_shared, x_shared, px_send, px_recv, partner).wait()

    width = 512

    def dense_step(step, carry):
        columns = pl.ds(pl.multiple_of(step * width, width), width)
        product = lax.dot_general(
            x_all[:, columns], k_cat[...], (((0,), (0,)), ((), ())), preferred_element_type=f32
        ).astype(bf16)
        for head in range(2):
            rows = pl.ds(head * DENSE_STRIDE + PER + step * (width // UNIT), width // UNIT)
            dense[rows] = product[:, head * 128:head * 128 + 128].reshape(width // UNIT, UNIT, HEAD_WIDTH)
        return carry

    lax.fori_loop(0, MODEL_WIDTH // width, dense_step, 0)

    def pick(ob):
        for oa in OFFSETS:
            y_ = a_at[oa] + core * (b_at[ob] - a_at[oa])
            z_ = b_at[ob] + core * (a_at[oa] - b_at[ob])
            head = z_ // 4
            first = y_ * 48 + lax.rem(z_, 4) * 12 + core * SHARD_UNITS
            for n in range(3):
                pair = first // 2 + n
                row = kept[head * 4 + xx, pair // 4]
                unit = head * DENSE_STRIDE + (row + 1) * PER + lax.rem(pair, 4) * 2
                for u in range(2):
                    rows = pl.ds(n * 32 + u * UNIT, UNIT)
                    part[AT[ob], AT[oa], rows] = dense[unit + u]

    def r_copy(oa, i, d, step):
        dest = 4 if step == 0 else d * (4 - step)
        ref, land = part.at[AT[dest], AT[oa]], got.at[AT[oa], i, step]
        if step == 0:
            ref, land = ref.at[pl.ds(i * HALF, HALF)], land.at[pl.ds(i * HALF, HALF)]
        return remote(ref, land, r_send.at[AT[oa], i, step], r_recv.at[AT[oa], i, step], to_b[d])

    def s_copy(i, d, step):
        ref, land = send2.at[i, step], got2.at[i, step]
        if step == 0:
            ref, land = ref.at[pl.ds(i * HALF, HALF)], land.at[pl.ds(i * HALF, HALF)]
        return remote(ref, land, s_send.at[i, step], s_recv.at[i, step], to_a[d])

    REDUCE = (4, 3, -3, 2, -2, 1, -1, 0)

    def r_step(step):
        for oa in REDUCE:
            for i, d in DIRECTIONS:
                if step:
                    r_copy(oa, i, d, step - 1).wait_recv()
                    rows = pl.ds(i * HALF, HALF) if step == 1 else pl.ds(0, SHARD)
                    m = AT[d * (4 - step)]
                    part[m, AT[oa], rows] = (
                        part[m, AT[oa], rows].astype(f32) + got[AT[oa], i, step - 1, rows].astype(f32)
                    ).astype(bf16)
                r_copy(oa, i, d, step).start()

    def r_last(oa):
        for i, d in DIRECTIONS:
            r_copy(oa, i, d, 3).wait_recv()
        j = AT[oa]
        total[j] = part[0, j].astype(f32) + got[j, 0, 3].astype(f32) + got[j, 1, 3].astype(f32)

    def s_step(step):
        for i, d in DIRECTIONS:
            if step == 0:
                rows = pl.ds(i * HALF, HALF)
                send2[i, 0, rows] = total[AT[4], rows].astype(bf16)
            else:
                s_copy(i, d, step - 1).wait_recv()
                j = AT[d * (4 - step)]
                if step == 1:
                    rows, rest = pl.ds(i * HALF, HALF), pl.ds((1 - i) * HALF, HALF)
                    send2[i, 1, rows] = (total[j, rows] + got2[i, 0, rows].astype(f32)).astype(bf16)
                    send2[i, 1, rest] = total[j, rest].astype(bf16)
                else:
                    send2[i, step] = (total[j] + got2[i, step - 1].astype(f32)).astype(bf16)
            s_copy(i, d, step).start()

    k_own = pl.ds(pl.multiple_of(core * 64, 64), 64)

    def block_at(head, row):
        unit = head * HEAD_STRIDE + slot_of[head * 4 + xx, row] * PER
        return jnp.concatenate([w_all[unit + u] for u in range(PER)], axis=0)

    def input_group(group):
        def body(step, carry):
            row = group * 16 + step * 2
            blocks = [
                jnp.concatenate([block_at(0, row + n), block_at(1, row + n)], axis=1) for n in range(2)
            ]
            product = lax.dot_general(
                k_cat[k_own, :], jnp.concatenate(blocks, axis=0), (((1,), (1,)), ((), ())),
                preferred_element_type=f32,
            )
            og[:, pl.ds(pl.multiple_of(row * BLOCK, 256), 256)] = product.astype(bf16)
            return carry

        lax.fori_loop(0, 8, body, 0)

    def own_rows(offset):
        return pl.ds(pl.multiple_of(wrap(xx + offset, XN) * OWN, OWN), OWN)

    def o_copy(i, d, n):
        group = (2 * i + n % 2) if n < 2 or n >= 4 else (2 * (1 - i) + n % 2)
        if n < 2:
            src = og.at[own_rows(2), x_columns(group)]
            dst = xa.at[i, :, x_columns(n)]
        else:
            src = og.at[own_rows(d), x_columns(group)]
            dst = xr.at[i, :, x_columns(group)]
        return remote(src, dst, o_send.at[i, n], o_recv.at[i, n], to_x[d])

    def send_group(group):
        far, n = group // 2, group % 2
        i, d = DIRECTIONS[far]
        o_copy(i, d, n).start()
        i, d = DIRECTIONS[1 - far]
        o_copy(i, d, 2 + n).start()

    def forward_group(n):
        for i, d in DIRECTIONS:
            o_copy(i, d, n).wait_recv()
            columns = x_columns(2 * i + n)
            og[own_rows(d), columns] = (
                og[own_rows(d), columns].astype(f32) + xa[i, :, x_columns(n)].astype(f32)
            ).astype(bf16)
            o_copy(i, d, 4 + n).start()

    pick(4)
    r_step(0)
    for offset in (3, -3, 2, -2, 1, -1, 0):
        pick(offset)
    w_shared = w_all.at[pl.ds(0, HEAD_UNITS)]
    remote(w_shared, w_shared, pw_send, pw_recv, partner).wait()
    r_step(1)

    input_group(0)
    send_group(0)
    input_group(2)
    send_group(2)
    r_step(2)
    input_group(1)
    send_group(1)
    input_group(3)
    send_group(3)
    forward_group(0)
    r_step(3)
    forward_group(1)
    r_last(4)
    s_step(0)
    r_last(3)
    r_last(-3)
    r_last(2)
    r_last(-2)
    s_step(1)
    r_last(1)
    r_last(-1)
    s_step(2)
    r_last(0)
    s_step(3)
    for n in (2, 3, 4, 5):
        for i, d in DIRECTIONS:
            o_copy(i, d, n).wait_recv()
    mine = own_rows(0)

    def finish(step, carry):
        columns = pl.ds(pl.multiple_of(step * 512, 512), 512)
        x_out[:, columns] = (
            og[mine, columns].astype(f32) + xr[0, :, columns].astype(f32) + xr[1, :, columns].astype(f32)
        ).astype(bf16)
        return carry

    lax.fori_loop(0, MODEL_WIDTH // 512, finish, 0)
    for i, d in DIRECTIONS:
        s_copy(i, d, 3).wait_recv()
    scale = 1.0 / math.sqrt(MICRO * 4096)
    w_out[...] = (total[0] + got2[0, 3].astype(f32) + got2[1, 3].astype(f32)) * scale

    for i, d in DIRECTIONS:
        for step in range(4):
            a_copy(i, d, step + 1).wait_send()
            k_copy(i, d, step + 1).wait_send()
            s_copy(i, d, step).wait_send()
            for oa in OFFSETS:
                b_copy(oa, i, d, step + 1).wait_send()
                r_copy(oa, i, d, step).wait_send()
        for n in range(6):
            x_copy(i, d, n).wait_send()
            o_copy(i, d, n).wait_send()


def local(layer_input, key_gradient_rows, key_block_matrix, kept_rows):
    numbers = jnp.arange(1, SLOTS + 1, dtype=jnp.int32)[None, :, None]
    blocks = jnp.arange(BLOCKS, dtype=jnp.int32)[None, None, :]
    slot_of = jnp.sum(jnp.where(kept_rows[:, :, None] == blocks, numbers, 0), axis=1)
    any_space = pl.BlockSpec(memory_space=pl.ANY)
    vmem = pl.BlockSpec(memory_space=pltpu.VMEM)
    dma = pltpu.SemaphoreType.DMA
    weight_grad, input_grad = pl.pallas_call(
        kernel,
        out_shape=(
            jax.ShapeDtypeStruct((SHARD, HEAD_WIDTH), f32),
            jax.ShapeDtypeStruct((OWN, MODEL_WIDTH), bf16),
        ),
        in_specs=[pl.BlockSpec(memory_space=pltpu.SMEM), pl.BlockSpec(memory_space=pltpu.SMEM), any_space, any_space, any_space],
        out_specs=(vmem, vmem),
        scratch_shapes=[
            pltpu.VMEM((2 * HEAD_STRIDE, UNIT, HEAD_WIDTH), bf16),
            pltpu.VMEM((128, MODEL_WIDTH), bf16),
            pltpu.VMEM((2, 2, MICRO, 32, HEAD_WIDTH), bf16),
            pltpu.VMEM((2, 3, 32, HEAD_WIDTH), bf16),
            pltpu.VMEM((128, 2 * HEAD_WIDTH), bf16),
            pltpu.VMEM((2 * DENSE_STRIDE, UNIT, HEAD_WIDTH), bf16),
            pltpu.VMEM((N, N, SHARD, HEAD_WIDTH), bf16),
            pltpu.VMEM((N, 2, 4, SHARD, HEAD_WIDTH), bf16),
            pltpu.VMEM((N, SHARD, HEAD_WIDTH), f32),
            pltpu.VMEM((2, 4, SHARD, HEAD_WIDTH), bf16),
            pltpu.VMEM((2, 4, SHARD, HEAD_WIDTH), bf16),
            pltpu.VMEM((64, MODEL_WIDTH), bf16),
            pltpu.VMEM((2, OWN, MODEL_WIDTH), bf16),
            pltpu.VMEM((2, OWN, MODEL_WIDTH // 2), bf16),
            dma((3,)),
            dma((2, 4)), dma((2, 4)), dma((N, 2, 4)), dma((N, 2, 4)),
            dma, dma, dma, dma, dma((2,)), dma((2,)),
            dma((2, 6)), dma((2, 6)), dma((2, 4)), dma((2, 4)),
            dma((N, 2, 4)), dma((N, 2, 4)), dma((2, 4)), dma((2, 4)), dma((2, 6)), dma((2, 6)),
        ],
        compiler_params=pltpu.CompilerParams(collective_id=0, has_side_effects=True),
    )(
        kept_rows,
        slot_of,
        layer_input.reshape(OWN, MODEL_WIDTH),
        key_gradient_rows,
        key_block_matrix.reshape(SHARD_UNITS, UNIT, HEAD_WIDTH),
    )
    return (
        weight_grad.reshape(1, SHARD, HEAD_WIDTH),
        input_grad.reshape(MICRO, OWN // MICRO, MODEL_WIDTH),
    )


def solution(mesh):
    placed = (
        P(None, ("dp", "tensor"), None),
        P(None, "dp", "tensor"),
        P("tensor", "dp", None),
        P(),
    )
    return jax.shard_map(
        local,
        mesh=mesh,
        in_specs=placed,
        out_specs=(P("tensor", "dp", None), P(None, ("dp", "tensor"), None)),
        check_vma=False,
    )
```

time: 562 us -> 85.6 us (0.15)
  waiting for transfers between devices: 484 us -> 0 us
  Pallas kernels: 0 us -> 79 us
  local copies, waits for them, and re-layouts: 27.4 us -> 3.76 us
  other arithmetic: 17.2 us -> 0.73 us
  between operations: 14 us -> 0.65 us
  starting transfers between devices: 13.3 us -> 0 us
  matrix products: 5.81 us -> 0 us
    all_gather x3 -> x0, waiting for transfers between devices: 245 us -> none  [the longest x2 136 us: local(): group_x = lax.all_gather(layer_input[micro], 'tensor', axis=0, tiled=True)]
    reduce_scatter x1 -> x0, waiting for transfers between devices: 219 us -> none  [local(): lax.psum_scatter(accum.reshape(HEAD_BLOCK_LIMIT * PRUNE_BLOCK_ROWS, HEAD_...]
    pallas_call x0 -> x1, Pallas kernels: none -> 79 us  [local(): pl.pallas_call(kernel, out_shape=(jax.ShapeDtypeStruct((SHARD, HEAD_WIDTH...]
    all_to_all x2 -> x0, waiting for transfers between devices: 18.1 us -> none  [local(): lax.all_to_all(partial_value, 'tensor', split_axis=0, concat_axis=1, tile...]
    all_to_all x2 -> x0, starting transfers between devices: 13.1 us -> none  [local(): lax.all_to_all(partial_value, 'tensor', split_axis=0, concat_axis=1, tile...]
    reshape x2 -> x0, other arithmetic: 11.6 us -> none  [local(): partial_value.reshape(grads_here.shape[0], 1, HEAD_BLOCK_LIMIT * PRUNE_BL...]
    reshape x5 -> x0, local copies, waits for them, and re-layouts: 10.8 us -> none  [the longest x3 9.4 us: local(): partial_value.reshape(grads_here.shape[0], 1, HEAD_BLOCK_LIMIT * PRUNE_BL...]
    unnamed x12 -> x4, local copies, waits for them, and re-layouts: 10.6 us -> 3.76 us
  transfers between devices with their start and end apart: 6 -> 0, of which waited for: 6 -> 0; matrix products, arithmetic and copies ran while one was open for 8% -> 0% of each run, Pallas kernels for 0% -> 0%
where the time goes in v1:
time: 85.6 us; the launch traced here: 84.1 us
  Pallas kernels  79 us (92%)
  local copies, waits for them, and re-layouts  3.76 us (4%)
    pallas_call x1, Pallas kernels, local(): pl.pallas_call(kernel, out_shape=(jax.ShapeDtypeStruct((SHARD, HEAD_WIDTH...  79 us
    unnamed x4, local copies, waits for them, and re-layouts  3.76 us

profile of v1, /device:TPU:6, one launch (start us, length us, event | category | flops | bytes accessed | tf_op | source)
XLA Modules:
  0.0 84.1 jit_solution(12403357187883215349)
XLA Ops:
  0.6 0.0 copy-start
  0.7 0.7 copy-done
  1.3 0.7 select_reduce_fusion.slot_of
  2.0 79.0 %shard_map.59 = (f32[96,128]{1,0:T(8,128)}, bf16[16,8192]{1,0:T(8,128)(2,1)}) custom-call(s32[8,48]{1,0:T(8,128)} %kept.1, s32[8,64]{1,0:T(8,128)} %select_reduce_fusion.slot_of, bf16[16,8192]{1,0:T(8,128)(2,1)} %bitcast.4, bf16[2,64,128]{2,1,0:T(8,128)(2,1)} %k_in.1, bf16[6,16,128]{2,1,0:T(8,128)(2,1)} %bitcast.7), custom_call_target="tpu_custom_call" | custom-call | tf_op jit(solution)/shard_map/pallas_call | solution.py:439
  81.1 1.4 %copy.8 = f32[1,96,128]{2,1,0:T(8,128)} copy(f32[1,96,128]{2,1,0:T(8,128)} %bitcast.6) | data formatting | bytes 98304
  82.5 1.7 %copy.9 = bf16[2,8,8192]{2,1,0:T(8,128)(2,1)} copy(bf16[2,8,8192]{2,1,0:T(8,128)(2,1)} %bitcast.5) | data formatting | bytes 524288
  (1 shorter events, 0.0 us)
Async XLA Ops:
  0.6 0.7 copy-start

commit v2 on v1

--- a/solution.py
+++ b/solution.py
@@ -39,7 +39,7 @@
 
 def kernel(
     kept, slot_of, x_in, k_in, w_in, w_out, x_out,
-    w_all, x_all, k_raw, k_hop, k_cat, dense, part, got, total, got2, send2, og, xr, xa,
+    w_all, x_all, k_raw, k_cat, dense, part, got, total, got2, send2, og, xr, xa,
     local_sem, a_send, a_recv, b_send, b_recv, pw_send, pw_recv, px_send, px_recv, pk_send, pk_recv,
     x_send, x_recv, kc_send, kc_recv, r_send, r_recv, s_send, s_recv, o_send, o_recv,
 ):
@@ -67,15 +67,15 @@
 
     a_rows = {o: y_rows(v) + core * (z_rows(v) - y_rows(v)) + core * SHARD_UNITS for o, v in a_at.items()}
     b_rows = {o: z_rows(v) + core * (y_rows(v) - z_rows(v)) for o, v in b_at.items()}
-    to_a = {d: device_ab(a_at[d], b) for d in (1, -1)}
+    to_a = {o: device_ab(a_at[o], b) for o in OFFSETS if o}
     to_b = {d: device_ab(a, b_at[d]) for d in (1, -1)}
-    to_z = {d: device(y, wrap(z + d, N), core, xx) for d in (1, -1)}
+    far_z = device(y, wrap(z + 4, N), core, xx)
     to_x = {d: device(y, z, core, wrap(xx + d, XN)) for d in (1, -1)}
-    to_y = {d: device(wrap(y + d, N), z, core, xx) for d in (1, -1)}
     partner = device(y, z, 1 - core, xx)
 
     barrier = pltpu.get_barrier_semaphore()
-    for there in (to_y[1], to_y[-1], to_z[1], to_z[-1], to_x[1], to_x[-1], partner):
+    everyone = (*to_a.values(), *to_b.values(), *to_x.values(), partner, far_z)
+    for there in everyone:
         pl.semaphore_signal(barrier, inc=1, device_id=there, device_id_type=MESH)
 
     def remote(src, dst, send, recv, there):
@@ -89,14 +89,8 @@
             return w_all.at[pl.ds(row, SHARD_UNITS)]
         return w_all.at[pl.ds(row + half * (SHARD_UNITS // 2), SHARD_UNITS // 2)]
 
-    def ring_offset(d, hop):
-        return 4 if hop == 4 else -d * hop
-
-    def a_copy(i, d, hop):
-        offset = -d * (hop - 1)
-        half = i if hop == 4 else None
-        src = w_in if hop == 1 else piece(offset, 0, half)
-        return remote(src, piece(offset, 0, half), a_send.at[i, hop - 1], a_recv.at[i, hop - 1], to_a[d])
+    def a_copy(o):
+        return remote(w_in, piece(0, 0), a_send.at[AT[o]], a_recv.at[AT[o]], to_a[o])
 
     def b_copy(oa, i, d, hop):
         offset = -d * (hop - 1)
@@ -133,16 +127,9 @@
         ref = x_all.at[x_rows(core, origin), x_columns(X_ORDER[i][n])]
         remote(ref, ref, px_send, px_recv, partner).start()
 
-    def k_copy(i, d, hop):
-        if hop == 1:
-            src = k_in.at[i, pl.ds(pl.multiple_of((1 - zh) * 32, 32), 32)]
-        else:
-            src = k_hop.at[i, hop - 2]
-        if hop == 4:
-            dst = k_raw.at[core, 1 - wrap(z + d, N) // 4, i]
-        else:
-            dst = k_hop.at[i, hop - 1]
-        return remote(src, dst, kc_send.at[i, hop - 1], kc_recv.at[i, hop - 1], to_z[d])
+    def k_copy():
+        src = k_in.at[:, pl.ds(pl.multiple_of((1 - zh) * 32, 32), 32)]
+        return remote(src, k_raw.at[core, zh], kc_send, kc_recv, far_z)
 
     def k_share(own):
         if own:
@@ -164,12 +151,15 @@
         w_all[pl.ds(head * HEAD_STRIDE, PER)] = jnp.zeros((PER, UNIT, HEAD_WIDTH), bf16)
         dense[pl.ds(head * DENSE_STRIDE, PER)] = jnp.zeros((PER, UNIT, HEAD_WIDTH), bf16)
 
-    pl.semaphore_wait(barrier, 7)
-
+    pl.semaphore_wait(barrier, len(everyone))
+
+    for o in (1, -1):
+        a_copy(o).start()
     for i, d in DIRECTIONS:
-        a_copy(i, d, 1).start()
         b_copy(0, i, d, 1).start()
-        k_copy(i, d, 1).start()
+    k_copy().start()
+    for o in (2, -2, 3, -3, 4):
+        a_copy(o).start()
     for n in range(4):
         for i, d in DIRECTIONS:
             x_copy(i, d, n).start()
@@ -177,18 +167,11 @@
     k_share(True).start()
     remote(x_in, x_all.at[x_rows(core, xx)], px_send, px_recv, partner).start()
 
-    def a_arrival(step):
-        for i, d in DIRECTIONS:
-            a_copy(i, d, step).wait_recv()
-            if step < 4:
-                a_copy(i, d, step + 1).start()
-                for i2, d2 in DIRECTIONS:
-                    b_copy(-d * step, i2, d2, 1).start()
-                share(-d * step, 0)
-        if step == 4:
-            for i2, d2 in DIRECTIONS:
-                b_copy(4, i2, d2, 1).start()
-            share(4, 0)
+    def a_arrival(oa):
+        a_copy(-oa if oa != 4 else 4).wait_recv()
+        for i, d in DIRECTIONS:
+            b_copy(oa, i, d, 1).start()
+        share(oa, 0)
 
     def b_arrival(oa, hop):
         for i, d in DIRECTIONS:
@@ -199,31 +182,28 @@
             else:
                 share(oa, 4, i)
 
-    for step in range(1, 9):
-        if step <= 4:
-            a_arrival(step)
-        for oa in OFFSETS:
-            hop = step - abs(oa)
-            if 1 <= hop <= 4:
-                b_arrival(oa, hop)
-        if step <= 4:
-            for i, d in DIRECTIONS:
-                k_copy(i, d, step).wait_recv()
-                if step < 4:
-                    k_copy(i, d, step + 1).start()
-            if step == 4:
-                k_share(False).start()
-        if step in (2, 3, 5, 6):
-            n = {2: 0, 3: 1, 5: 2, 6: 3}[step]
-            for i, d in DIRECTIONS:
-                x_copy(i, d, n).wait_recv()
-                if n < 2:
-                    x_copy(i, d, n + 4).start()
-                share_x(i, d, n)
-    for n in (4, 5):
+    def x_arrival(n):
         for i, d in DIRECTIONS:
             x_copy(i, d, n).wait_recv()
+            if n < 2:
+                x_copy(i, d, n + 4).start()
             share_x(i, d, n)
+
+    def k_arrival():
+        k_copy().wait_recv()
+        k_share(False).start()
+
+    events = [(5.2, k_arrival, ())]
+    for n in range(6):
+        events.append((4.2 + 1.45 * n, x_arrival, (n,)))
+    for oa in OFFSETS:
+        first = 2.4 + 0.9 * abs(oa) if oa else 0.0
+        if oa:
+            events.append((first, a_arrival, (oa,)))
+        for hop in range(1, 5):
+            events.append((first + 3.0 * hop, b_arrival, (oa, hop)))
+    for _, event, arguments in sorted(events, key=lambda entry: entry[0]):
+        event(*arguments)
 
     for copy in local:
         copy.wait()
@@ -274,11 +254,8 @@
             ref, land = ref.at[pl.ds(i * HALF, HALF)], land.at[pl.ds(i * HALF, HALF)]
         return remote(ref, land, r_send.at[AT[oa], i, step], r_recv.at[AT[oa], i, step], to_b[d])
 
-    def s_copy(i, d, step):
-        ref, land = send2.at[i, step], got2.at[i, step]
-        if step == 0:
-            ref, land = ref.at[pl.ds(i * HALF, HALF)], land.at[pl.ds(i * HALF, HALF)]
-        return remote(ref, land, s_send.at[i, step], s_recv.at[i, step], to_a[d])
+    def s_copy(o):
+        return remote(send2.at[AT[o]], got2.at[AT[o]], s_send.at[AT[o]], s_recv.at[AT[o]], to_a[o])
 
     REDUCE = (4, 3, -3, 2, -2, 1, -1, 0)
 
@@ -298,23 +275,12 @@
         for i, d in DIRECTIONS:
             r_copy(oa, i, d, 3).wait_recv()
         j = AT[oa]
-        total[j] = part[0, j].astype(f32) + got[j, 0, 3].astype(f32) + got[j, 1, 3].astype(f32)
-
-    def s_step(step):
-        for i, d in DIRECTIONS:
-            if step == 0:
-                rows = pl.ds(i * HALF, HALF)
-                send2[i, 0, rows] = total[AT[4], rows].astype(bf16)
-            else:
-                s_copy(i, d, step - 1).wait_recv()
-                j = AT[d * (4 - step)]
-                if step == 1:
-                    rows, rest = pl.ds(i * HALF, HALF), pl.ds((1 - i) * HALF, HALF)
-                    send2[i, 1, rows] = (total[j, rows] + got2[i, 0, rows].astype(f32)).astype(bf16)
-                    send2[i, 1, rest] = total[j, rest].astype(bf16)
-                else:
-                    send2[i, step] = (total[j] + got2[i, step - 1].astype(f32)).astype(bf16)
-            s_copy(i, d, step).start()
+        sums = part[0, j].astype(f32) + got[j, 0, 3].astype(f32) + got[j, 1, 3].astype(f32)
+        if oa:
+            send2[j] = sums.astype(bf16)
+            s_copy(oa).start()
+        else:
+            total[...] = sums
 
     k_own = pl.ds(pl.multiple_of(core * 64, 64), 64)
 
@@ -386,18 +352,8 @@
     forward_group(0)
     r_step(3)
     forward_group(1)
-    r_last(4)
-    s_step(0)
-    r_last(3)
-    r_last(-3)
-    r_last(2)
-    r_last(-2)
-    s_step(1)
-    r_last(1)
-    r_last(-1)
-    s_step(2)
-    r_last(0)
-    s_step(3)
+    for offset in REDUCE:
+        r_last(offset)
     for n in (2, 3, 4, 5):
         for i, d in DIRECTIONS:
             o_copy(i, d, n).wait_recv()
@@ -411,16 +367,18 @@
         return carry
 
     lax.fori_loop(0, MODEL_WIDTH // 512, finish, 0)
-    for i, d in DIRECTIONS:
-        s_copy(i, d, 3).wait_recv()
-    scale = 1.0 / math.sqrt(MICRO * 4096)
-    w_out[...] = (total[0] + got2[0, 3].astype(f32) + got2[1, 3].astype(f32)) * scale
-
+    sums = total[...]
+    for o in OFFSETS[1:]:
+        s_copy(o).wait_recv()
+        sums = sums + got2[AT[o]].astype(f32)
+    w_out[...] = sums * (1.0 / math.sqrt(MICRO * 4096))
+
+    k_copy().wait_send()
+    for o in OFFSETS[1:]:
+        a_copy(o).wait_send()
+        s_copy(o).wait_send()
     for i, d in DIRECTIONS:
         for step in range(4):
-            a_copy(i, d, step + 1).wait_send()
-            k_copy(i, d, step + 1).wait_send()
-            s_copy(i, d, step).wait_send()
             for oa in OFFSETS:
                 b_copy(oa, i, d, step + 1).wait_send()
                 r_copy(oa, i, d, step).wait_send()
@@ -448,22 +406,21 @@
             pltpu.VMEM((2 * HEAD_STRIDE, UNIT, HEAD_WIDTH), bf16),
             pltpu.VMEM((128, MODEL_WIDTH), bf16),
             pltpu.VMEM((2, 2, MICRO, 32, HEAD_WIDTH), bf16),
-            pltpu.VMEM((2, 3, 32, HEAD_WIDTH), bf16),
             pltpu.VMEM((128, 2 * HEAD_WIDTH), bf16),
             pltpu.VMEM((2 * DENSE_STRIDE, UNIT, HEAD_WIDTH), bf16),
             pltpu.VMEM((N, N, SHARD, HEAD_WIDTH), bf16),
             pltpu.VMEM((N, 2, 4, SHARD, HEAD_WIDTH), bf16),
-            pltpu.VMEM((N, SHARD, HEAD_WIDTH), f32),
-            pltpu.VMEM((2, 4, SHARD, HEAD_WIDTH), bf16),
-            pltpu.VMEM((2, 4, SHARD, HEAD_WIDTH), bf16),
+            pltpu.VMEM((SHARD, HEAD_WIDTH), f32),
+            pltpu.VMEM((N, SHARD, HEAD_WIDTH), bf16),
+            pltpu.VMEM((N, SHARD, HEAD_WIDTH), bf16),
             pltpu.VMEM((64, MODEL_WIDTH), bf16),
             pltpu.VMEM((2, OWN, MODEL_WIDTH), bf16),
             pltpu.VMEM((2, OWN, MODEL_WIDTH // 2), bf16),
             dma((3,)),
-            dma((2, 4)), dma((2, 4)), dma((N, 2, 4)), dma((N, 2, 4)),
+            dma((N,)), dma((N,)), dma((N, 2, 4)), dma((N, 2, 4)),
             dma, dma, dma, dma, dma((2,)), dma((2,)),
-            dma((2, 6)), dma((2, 6)), dma((2, 4)), dma((2, 4)),
-            dma((N, 2, 4)), dma((N, 2, 4)), dma((2, 4)), dma((2, 4)), dma((2, 6)), dma((2, 6)),
+            dma((2, 6)), dma((2, 6)), dma, dma,
+            dma((N, 2, 4)), dma((N, 2, 4)), dma((N,)), dma((N,)), dma((2, 6)), dma((2, 6)),
         ],
         compiler_params=pltpu.CompilerParams(collective_id=0, has_side_effects=True),
     )(

time: 85.6 us -> 70.3 us (0.82)
  Pallas kernels: 79 us -> 64.4 us
    pallas_call x1, Pallas kernels: 79 us -> 64.4 us  [local(): pl.pallas_call(kernel, out_shape=(jax.ShapeDtypeStruct((SHARD, HEAD_WIDTH...]
where the time goes in v2:
time: 70.3 us; the launch traced here: 69.5 us
  Pallas kernels  64.4 us (92%)
  local copies, waits for them, and re-layouts  3.76 us (5%)
  other arithmetic  0.73 us (1%)
    pallas_call x1, Pallas kernels, local(): pl.pallas_call(kernel, out_shape=(jax.ShapeDtypeStruct((SHARD, HEAD_WIDTH...  64.4 us
    unnamed x4, local copies, waits for them, and re-layouts  3.76 us

profile of v2, /device:TPU:6, one launch (start us, length us, event | category | flops | bytes accessed | tf_op | source)
XLA Modules:
  0.0 69.5 jit_solution(15668816873213667965)
XLA Ops:
  0.6 0.0 copy-start
  0.7 0.7 copy-done
  1.3 0.7 %select_reduce_fusion.slot_of = s32[8,64]{1,0:T(8,128)} fusion(s32[48]{0:T(128)S(1)} %iota_add_fusion, s32[8,48]{1,0:T(8,128)S(1)} %copy-done), kind=kLoop, calls=%fused_computation | loop fusion | flops 73216 | bytes 3776 | tf_op jit(solution)/shard_map/reduce_sum | solution.py:393
  2.0 64.4 %shard_map.59 = (f32[96,128]{1,0:T(8,128)}, bf16[16,8192]{1,0:T(8,128)(2,1)}) custom-call(s32[8,48]{1,0:T(8,128)} %kept.1, s32[8,64]{1,0:T(8,128)} %select_reduce_fusion.slot_of, bf16[16,8192]{1,0:T(8,128)(2,1)} %bitcast.4, bf16[2,64,128]{2,1,0:T(8,128)(2,1)} %k_in.1, bf16[6,16,128]{2,1,0:T(8,128)(2,1)} %bitcast.7), custom_call_target="tpu_custom_call" | custom-call | tf_op jit(solution)/shard_map/pallas_call | solution.py:397
  66.4 1.4 %copy.8 = f32[1,96,128]{2,1,0:T(8,128)} copy(f32[1,96,128]{2,1,0:T(8,128)} %bitcast.6) | data formatting | bytes 98304
  67.8 1.7 %copy.9 = bf16[2,8,8192]{2,1,0:T(8,128)(2,1)} copy(bf16[2,8,8192]{2,1,0:T(8,128)(2,1)} %bitcast.5) | data formatting | bytes 524288
  (1 shorter events, 0.0 us)
Async XLA Ops:
  0.6 0.7 copy-start

commit v3 on v2

--- a/solution.py
+++ b/solution.py
@@ -29,6 +29,7 @@
 OFFSETS = (0, 1, -1, 2, -2, 3, -3, 4)
 AT = {offset: index for index, offset in enumerate(OFFSETS)}
 DIRECTIONS = ((0, 1), (1, -1))
+HOP, T_D, T_R, T_I = 3.3, 13.2, 15.9, 20.5
 X_ORDER = ((0, 1, 2, 3, 0, 1), (2, 3, 0, 1, 2, 3))
 f32, bf16 = jnp.float32, jnp.bfloat16
 
@@ -193,31 +194,20 @@
         k_copy().wait_recv()
         k_share(False).start()
 
-    events = [(5.2, k_arrival, ())]
-    for n in range(6):
-        events.append((4.2 + 1.45 * n, x_arrival, (n,)))
-    for oa in OFFSETS:
-        first = 2.4 + 0.9 * abs(oa) if oa else 0.0
-        if oa:
-            events.append((first, a_arrival, (oa,)))
-        for hop in range(1, 5):
-            events.append((first + 3.0 * hop, b_arrival, (oa, hop)))
-    for _, event, arguments in sorted(events, key=lambda entry: entry[0]):
-        event(*arguments)
-
-    for copy in local:
-        copy.wait()
-    k_share(True).wait()
-    k_share(False).wait()
-    for core_ in range(2):
-        for head in range(2):
-            raw = k_raw[core_, head].astype(f32)
-            rows = [raw[m, x_ * 8:x_ * 8 + 8] for x_ in range(XN) for m in range(MICRO)]
-            k_cat[core_ * 64:core_ * 64 + 64, head * 128:head * 128 + 128] = jnp.concatenate(
-                rows, axis=0
-            ).astype(bf16)
-    x_shared = x_all.at[pl.ds(0, 64)]
-    remote(x_shared, x_shared, px_send, px_recv, partner).wait()
+    def prepare():
+        for copy in local:
+            copy.wait()
+        k_share(True).wait()
+        k_share(False).wait()
+        for core_ in range(2):
+            for head in range(2):
+                raw = k_raw[core_, head].astype(f32)
+                rows = [raw[m, x_ * 8:x_ * 8 + 8] for x_ in range(XN) for m in range(MICRO)]
+                k_cat[core_ * 64:core_ * 64 + 64, head * 128:head * 128 + 128] = jnp.concatenate(
+                    rows, axis=0
+                ).astype(bf16)
+        x_shared = x_all.at[pl.ds(0, 64)]
+        remote(x_shared, x_shared, px_send, px_recv, partner).wait()
 
     width = 512
 
@@ -231,9 +221,15 @@
             dense[rows] = product[:, head * 128:head * 128 + 128].reshape(width // UNIT, UNIT, HEAD_WIDTH)
         return carry
 
-    lax.fori_loop(0, MODEL_WIDTH // width, dense_step, 0)
-
-    def pick(ob):
+    def dense_part(part_):
+        steps = MODEL_WIDTH // width // 4
+        lax.fori_loop(part_ * steps, (part_ + 1) * steps, dense_step, 0, unroll=True)
+
+    def pick(*which):
+        for ob in which:
+            pick_one(ob)
+
+    def pick_one(ob):
         for oa in OFFSETS:
             y_ = a_at[oa] + core * (b_at[ob] - a_at[oa])
             z_ = b_at[ob] + core * (a_at[oa] - b_at[ob])
@@ -259,8 +255,8 @@
 
     REDUCE = (4, 3, -3, 2, -2, 1, -1, 0)
 
-    def r_step(step):
-        for oa in REDUCE:
+    def r_step(step, which):
+        for oa in which:
             for i, d in DIRECTIONS:
                 if step:
                     r_copy(oa, i, d, step - 1).wait_recv()
@@ -301,7 +297,7 @@
             og[:, pl.ds(pl.multiple_of(row * BLOCK, 256), 256)] = product.astype(bf16)
             return carry
 
-        lax.fori_loop(0, 8, body, 0)
+        lax.fori_loop(0, 8, body, 0, unroll=True)
 
     def own_rows(offset):
         return pl.ds(pl.multiple_of(wrap(xx + offset, XN) * OWN, OWN), OWN)
@@ -332,28 +328,54 @@
             ).astype(bf16)
             o_copy(i, d, 4 + n).start()
 
-    pick(4)
-    r_step(0)
-    for offset in (3, -3, 2, -2, 1, -1, 0):
-        pick(offset)
-    w_shared = w_all.at[pl.ds(0, HEAD_UNITS)]
-    remote(w_shared, w_shared, pw_send, pw_recv, partner).wait()
-    r_step(1)
-
-    input_group(0)
-    send_group(0)
-    input_group(2)
-    send_group(2)
-    r_step(2)
-    input_group(1)
-    send_group(1)
-    input_group(3)
-    send_group(3)
-    forward_group(0)
-    r_step(3)
-    forward_group(1)
-    for offset in REDUCE:
-        r_last(offset)
+    def blocks_complete():
+        w_shared = w_all.at[pl.ds(0, HEAD_UNITS)]
+        remote(w_shared, w_shared, pw_send, pw_recv, partner).wait()
+
+    def input_part(group):
+        input_group(group)
+        send_group(group)
+
+    events = [(5.2, k_arrival, ())]
+    for n in range(6):
+        events.append((4.2 + 1.45 * n, x_arrival, (n,)))
+    for oa in OFFSETS:
+        first = 2.4 + 0.9 * abs(oa) if oa else 0.0
+        if oa:
+            events.append((first, a_arrival, (oa,)))
+        for hop in range(1, 5):
+            events.append((first + HOP * hop, b_arrival, (oa, hop)))
+    near, rest = REDUCE[:4], REDUCE[4:]
+    events += [
+        (T_D, prepare, ()),
+        (T_D + 0.1, dense_part, (0,)),
+        (T_D + 0.7, dense_part, (1,)),
+        (T_D + 1.3, dense_part, (2,)),
+        (T_D + 1.9, dense_part, (3,)),
+        (T_R, pick, (4,)),
+        (T_R + 0.1, r_step, (0, REDUCE)),
+        (T_R + 0.5, pick, (3, -3)),
+        (T_R + 1.0, pick, (2, -2)),
+        (T_R + 1.5, pick, (1, -1, 0)),
+        (T_R + 2.9, r_step, (1, near)),
+        (T_R + 3.4, r_step, (1, rest)),
+        (T_R + 5.9, r_step, (2, near)),
+        (T_R + 6.6, r_step, (2, rest)),
+        (T_R + 9.0, r_step, (3, near)),
+        (T_R + 9.7, r_step, (3, rest)),
+        (T_I, blocks_complete, ()),
+        (T_I + 0.1, input_part, (0,)),
+        (T_I + 0.9, input_part, (2,)),
+        (T_I + 1.7, input_part, (1,)),
+        (T_I + 2.5, input_part, (3,)),
+        (T_I + 5.2, forward_group, (0,)),
+        (T_I + 7.5, forward_group, (1,)),
+    ]
+    for n, offset in enumerate(REDUCE):
+        events.append((T_R + 12.1 + 0.26 * n, r_last, (offset,)))
+    for _, event, arguments in sorted(events, key=lambda entry: entry[0]):
+        event(*arguments)
+
     for n in (2, 3, 4, 5):
         for i, d in DIRECTIONS:
             o_copy(i, d, n).wait_recv()

time: 70.3 us -> 61.2 us (0.87)
  Pallas kernels: 64.4 us -> 55 us
    pallas_call x1, Pallas kernels: 64.4 us -> 55 us  [local(): pl.pallas_call(kernel, out_shape=(jax.ShapeDtypeStruct((SHARD, HEAD_WIDTH...]
where the time goes in v3:
time: 61.2 us; the launch traced here: 60.1 us
  Pallas kernels  55 us (90%)
  local copies, waits for them, and re-layouts  3.76 us (6%)
  other arithmetic  0.73 us (1%)
  between operations  0.65 us (1%)
    pallas_call x1, Pallas kernels, local(): pl.pallas_call(kernel, out_shape=(jax.ShapeDtypeStruct((SHARD, HEAD_WIDTH...  55 us
    unnamed x4, local copies, waits for them, and re-layouts  3.76 us

profile of v3, /device:TPU:6, one launch (start us, length us, event | category | flops | bytes accessed | tf_op | source)
XLA Modules:
  0.0 60.1 jit_solution(11791881961062131963)
XLA Ops:
  0.6 0.0 copy-start
  0.7 0.7 %copy-done = s32[8,48]{1,0:T(8,128)S(1)} copy-done((s32[8,48]{1,0:T(8,128)S(1)}, s32[8,48]{1,0:T(8,128)}, u32[]{:S(2)}) %copy-start) | copy-done | bytes 1560
  1.3 0.7 %select_reduce_fusion.slot_of = s32[8,64]{1,0:T(8,128)} fusion(s32[48]{0:T(128)S(1)} %iota_add_fusion, s32[8,48]{1,0:T(8,128)S(1)} %copy-done), kind=kLoop, calls=%fused_computation | loop fusion | flops 73216 | bytes 3776 | tf_op jit(solution)/shard_map/reduce_sum | solution.py:415
  2.0 55.0 %shard_map.59 = (f32[96,128]{1,0:T(8,128)}, bf16[16,8192]{1,0:T(8,128)(2,1)}) custom-call(s32[8,48]{1,0:T(8,128)} %kept.1, s32[8,64]{1,0:T(8,128)} %select_reduce_fusion.slot_of, bf16[16,8192]{1,0:T(8,128)(2,1)} %bitcast.4, bf16[2,64,128]{2,1,0:T(8,128)(2,1)} %k_in.1, bf16[6,16,128]{2,1,0:T(8,128)(2,1)} %bitcast.7), custom_call_target="tpu_custom_call" | custom-call | tf_op jit(solution)/shard_map/pallas_call | solution.py:419
  57.0 1.4 %copy.8 = f32[1,96,128]{2,1,0:T(8,128)} copy(f32[1,96,128]{2,1,0:T(8,128)} %bitcast.6) | data formatting | bytes 98304
  58.4 1.7 %copy.9 = bf16[2,8,8192]{2,1,0:T(8,128)(2,1)} copy(bf16[2,8,8192]{2,1,0:T(8,128)(2,1)} %bitcast.5) | data formatting | bytes 524288
  (1 shorter events, 0.0 us)
Async XLA Ops:
  0.6 0.7 %copy-start = (s32[8,48]{1,0:T(8,128)S(1)}, s32[8,48]{1,0:T(8,128)}, u32[]{:S(2)}) copy-start(s32[8,48]{1,0:T(8,128)} %kept.1) | copy-start | bytes 4612
